TPU v7x, 128 devices: a whole 4x4x4 slice. The times are simulated.
128 devices in a mesh: lists: 8 (over z, core), seq: 16 (over y, x).
Axes of the slice: x: 4, y: 4, z: 4, core: 2. Of those that a mesh axis runs over, the one named last changes fastest.
Arguments:
- queries: bfloat16 [98304, 2048], P(('lists', 'seq')), parts along dimension 0, may hold values from -6 to 6
- key_rows: bfloat16 [98304, 2048], P(('lists', 'seq')), parts along dimension 0, may hold values from -6 to 6
- value_rows: bfloat16 [98304, 2048], P(('lists', 'seq')), parts along dimension 0, may hold values from -6 to 6
- out_grad: bfloat16 [98304, 2048], P(('lists', 'seq')), parts along dimension 0, may hold values from -6 to 6
Outputs:
- query_grad: bfloat16 [98304, 2048], P(('lists', 'seq')), parts along dimension 0
- key_grad: bfloat16 [98304, 2048], P(('lists', 'seq')), parts along dimension 0
- content_derivative: bfloat16 [98304, 2048], P(('lists', 'seq')), parts along dimension 0
There are 8 independent parts, one for each index of `lists`. A program takes and returns all parts, laid end to end along the dimension named above; each array names one. Nothing has to cross between parts.
All inputs are finite; a program needn't handle non-finite values.
Results may differ from a plain program's by a relative error of at most 0.0049.
Values sent between devices are 32-bit elements; how exact they have to be, the bound alone decides.
A program may use at most 192 MiB of HBM per device.

v0:
```python
import jax
import jax.numpy as jnp
from jax import lax
from jax.sharding import PartitionSpec as P

HEADS = 16
HEAD_DIM = 128


def carried_in(part, axis, combine, identity, reverse):
    count = lax.axis_size(axis)
    place = lax.axis_index(axis)
    ahead = count - 1 - place if reverse else place
    gathered = lax.all_gather(part, axis)
    state = jnp.zeros_like(part) + jnp.asarray(identity, part.dtype)

    def one(turn, state):
        source = count - 1 - turn if reverse else turn
        return combine(state, lax.dynamic_index_in_dim(gathered, source, 0, False))

    return lax.fori_loop(0, ahead, one, state)


def add_states(earlier, later_state):
    return earlier + later_state


def on_device(queries, key_rows, value_rows, out_grad):
    rows = queries.shape[0]
    length = rows * lax.axis_size("seq")
    scale_factor = (HEAD_DIM * length) ** (-0.5)
    shape3 = (rows, HEADS, HEAD_DIM)
    query_token_rows = queries.reshape(shape3)
    lookup_per_position = key_rows.reshape(shape3)
    content_per_position = value_rows.reshape(shape3)
    gradient_token_rows = out_grad.reshape(shape3)
    key_value_sum = jnp.einsum(
        "mjw,mjf->jwf",
        lookup_per_position,
        content_per_position,
        preferred_element_type=jnp.float32,
    )
    query_output_sum = jnp.einsum(
        "axo,axu->xou", query_token_rows, gradient_token_rows, preferred_element_type=jnp.float32
    )
    zero_state = jnp.zeros((HEADS, HEAD_DIM, HEAD_DIM), jnp.float32)
    cumulative_leading = carried_in(key_value_sum, "seq", add_states, zero_state, False)
    suffix = carried_in(query_output_sum, "seq", add_states, zero_state, True)
    prefix_halves = cumulative_leading.astype(jnp.bfloat16)
    suffix_halves = suffix.astype(jnp.bfloat16)
    counter = jnp.arange(rows, dtype=jnp.int32)
    causal = (counter[:, None] >= counter[None, :])[None]
    scores = jnp.einsum(
        "thk,shk->hts", query_token_rows, lookup_per_position, preferred_element_type=jnp.float32
    )
    forward_weight_matrix = jnp.where(causal, scale_factor * scores, 0.0).astype(jnp.bfloat16)
    products = jnp.einsum(
        "thv,shv->hts",
        gradient_token_rows,
        content_per_position,
        preferred_element_type=jnp.float32,
    )
    weight_gradients = jnp.where(causal, scale_factor * products, 0.0).astype(jnp.bfloat16)
    query_portion = jnp.einsum(
        "ynv,vyq->nyq", weight_gradients, lookup_per_position, preferred_element_type=jnp.float32
    )
    query_portion = query_portion + scale_factor * jnp.einsum(
        "aro,rbo->arb", gradient_token_rows, prefix_halves, preferred_element_type=jnp.float32
    )
    key_portion = jnp.einsum(
        "eca,ceo->aeo", weight_gradients, query_token_rows, preferred_element_type=jnp.float32
    )
    key_portion = key_portion + scale_factor * jnp.einsum(
        "jan,aon->jao", content_per_position, suffix_halves, preferred_element_type=jnp.float32
    )
    value_portion = jnp.einsum(
        "uno,nud->oud",
        forward_weight_matrix,
        gradient_token_rows,
        preferred_element_type=jnp.float32,
    )
    value_portion = value_portion + scale_factor * jnp.einsum(
        "nam,amx->nax", lookup_per_position, suffix_halves, preferred_element_type=jnp.float32
    )
    flat = (rows, HEADS * HEAD_DIM)
    return (
        query_portion.astype(jnp.bfloat16).reshape(flat),
        key_portion.astype(jnp.bfloat16).reshape(flat),
        value_portion.astype(jnp.bfloat16).reshape(flat),
    )


def solution(mesh):
    placed = (
        P(("lists", "seq"), None),
        P(("lists", "seq"), None),
        P(("lists", "seq"), None),
        P(("lists", "seq"), None),
    )
    return jax.shard_map(
        on_device,
        mesh=mesh,
        in_specs=placed,
        out_specs=(P(("lists", "seq"), None), P(("lists", "seq"), None), P(("lists", "seq"), None)),
        check_vma=False,
    )
```

profile of v0, /device:TPU:1, one launch (start us, length us, event | category | flops | bytes accessed | tf_op | source)
XLA Modules:
  0.0 323.1 jit_solution(12171814768745881696)
XLA Ops:
  9.1 4.2 %fusion.17 = f32[16,128,128]{2,1,0:T(8,128)} fusion(bf16[768,2048]{1,0:T(8,128)(2,1)S(1)} %copy-done, bf16[768,2048]{1,0:T(8,128)(2,1)} %param.9), kind=kOutput, calls=%fused_computation.21 | convolution fusion | flops 402653184 | bytes 7340032 | tf_op jit(solution)/shard_map/mjw,mjf->jwf/dot_general | solution.py:37
  13.4 4.6 %copy.41 = bf16[768,2048]{0,1:T(8,128)(2,1)} copy(bf16[768,2048]{1,0:T(8,128)(2,1)} %param.11) | data formatting | bytes 6291456 | tf_op jit(solution)/shard_map/reshape | solution.py:36
  18.0 4.9 %fusion.9 = f32[16,128,128]{2,1,0:T(8,128)} fusion(bf16[768,16,128]{0,2,1:T(8,128)(2,1)} %bitcast.102, bf16[768,2048]{1,0:T(8,128)(2,1)} %param.8), kind=kOutput, calls=%fused_computation.15 | convolution fusion | flops 402653184 | bytes 7340032 | tf_op jit(solution)/shard_map/axo,axu->xou/dot_general | solution.py:43
  23.9 11.8 %select_convert_fusion.1 = bf16[16,768,768]{2,1,0:T(8,128)(2,1)} fusion(pred[768,768]{1,0:T(8,128)(4,1)} %iota_compare_fusion, bf16[768,16,128]{0,2,1:T(8,128)(2,1)} %bitcast.103, bf16[768,2048]{1,0:T(8,128)(2,1)S(1)} %copy-done), kind=kOutput, calls=%fused_computation.3 | convolution fusion | flops 2444230656 | bytes 25755648 | tf_op jit(solution)/shard_map/thv,shv->hts/dot_general | solution.py:57
  35.7 13.3 %fusion.11 = f32[16,768,128]{1,2,0:T(8,128)} fusion(bf16[16,768,768]{2,1,0:T(8,128)(2,1)} %select_convert_fusion.1, bf16[768,2048]{1,0:T(8,128)(2,1)} %param.8), kind=kOutput, calls=%fused_computation.17 | convolution fusion | flops 2415919104 | bytes 28311552 | tf_op jit(solution)/shard_map/eca,ceo->aeo/dot_general | solution.py:70
  49.0 12.7 %fusion.19 = f32[16,768,128]{1,2,0:T(8,128)} fusion(bf16[16,768,768]{2,1,0:T(8,128)(2,1)} %select_convert_fusion.1, bf16[768,2048]{1,0:T(8,128)(2,1)} %param.9), kind=kOutput, calls=%fused_computation.23 | convolution fusion | flops 2415919104 | bytes 28311552 | tf_op jit(solution)/shard_map/ynv,vyq->nyq/dot_general | solution.py:64
  61.6 12.4 %fusion = f32[16,768,128]{1,2,0:T(8,128)} fusion(bf16[768,16,128]{0,2,1:T(8,128)(2,1)} %bitcast.104, pred[768,768]{1,0:T(8,128)(4,1)} %iota_compare_fusion, bf16[768,2048]{1,0:T(8,128)(2,1)} %param.8, bf16[768,2048]{1,0:T(8,128)(2,1)} %param.9), kind=kOutput, calls=%fused_computation.4 | convolution fusion | flops 4860149760 | bytes 16318464 | tf_op jit(solution)/shard_map/uno,nud->oud/dot_general | solution.py:76
  74.0 53.9 %all-gather.5.cloned.1.call-done = f32[256,128,128]{2,1,0:T(8,128)} async-done(((f32[16,128,128]{2,1,0:T(8,128)}), f32[256,128,128]{2,1,0:T(8,128)}) %all-gather.5.cloned.1.call-update) | async-done | bytes 16777232 | tf_op jit(solution)/shard_map/all_gather | solution.py:14
  129.0 112.5 %all-gather.7.cloned.1.call-done = f32[256,128,128]{2,1,0:T(8,128)} async-done(((f32[16,128,128]{2,1,0:T(8,128)}), f32[256,128,128]{2,1,0:T(8,128)}) %all-gather.7.cloned.1.call-update) | async-done | bytes 16777232 | tf_op jit(solution)/shard_map/all_gather | solution.py:14
  242.6 40.3 %while.23 = (s32[]{:T(128)}, f32[16,128,128]{2,1,0:T(8,128)}, s32[]{:T(128)}, f32[16,16,128,128]{3,2,1,0:T(8,128)}, s32[]{:T(128)}, /*index=5*/s32[]{:T(128)}, s32[]{:T(128)}, s32[]{:T(128)}) while((s32[]{:T(128)}, f32[16,128,128]{2,1,0:T(8,128)}, s32[]{:T(128)}, f32[16,16,128,128]{3,2,1,0:T(8,128)}, s32[]{:T(128)}, /*index=5*/s32[]{:T(128)}, ...), condition=%wide.region_3.4_spmd, body=%wide.region_2.3_spmd.sunk | while | flops 262150 | bytes 3145871 | solution.py:21
  242.6 2.7 bitcast_add_fusion.8
  248.0 2.7 bitcast_add_fusion.8
  250.7 2.7 bitcast_add_fusion.8
  253.4 2.7 bitcast_add_fusion.8
  264.1 2.7 bitcast_add_fusion.8
  266.8 2.7 bitcast_add_fusion.8
  269.5 2.7 bitcast_add_fusion.8
  272.2 2.7 bitcast_add_fusion.8
  282.9 6.9 %fusion.6 = bf16[768,16,128]{0,2,1:T(8,128)(2,1)} fusion(f32[16,768,128]{1,2,0:T(8,128)} %fusion, f32[16,128,128]{2,1,0:T(8,128)} %get-tuple-element.83, bf16[768,2048]{1,0:T(8,128)(2,1)} %param.9), kind=kOutput, calls=%fused_computation.10 | convolution fusion | flops 407633920 | bytes 13631488 | tf_op jit(solution)/shard_map/nam,amx->nax/dot_general | solution.py:82
  289.8 4.6 %copy.38 = bf16[768,2048]{1,0:T(8,128)(2,1)} copy(bf16[768,2048]{0,1:T(8,128)(2,1)} %bitcast.108) | data formatting | bytes 6291456
  294.5 5.8 %fusion.7 = bf16[768,16,128]{0,2,1:T(8,128)(2,1)} fusion(f32[16,768,128]{1,2,0:T(8,128)} %fusion.11, f32[16,128,128]{2,1,0:T(8,128)} %get-tuple-element.83, bf16[768,2048]{1,0:T(8,128)(2,1)S(1)} %copy-done), kind=kOutput, calls=%fused_computation.12 | convolution fusion | flops 407633920 | bytes 13631488 | tf_op jit(solution)/shard_map/jan,aon->jao/dot_general | solution.py:73
  300.3 4.6 %copy.37 = bf16[768,2048]{1,0:T(8,128)(2,1)} copy(bf16[768,2048]{0,1:T(8,128)(2,1)} %bitcast.107) | data formatting | bytes 6291456
  304.9 6.7 %fusion.8 = bf16[768,16,128]{0,2,1:T(8,128)(2,1)} fusion(f32[16,768,128]{1,2,0:T(8,128)} %fusion.19, bf16[768,16,128]{0,2,1:T(8,128)(2,1)} %bitcast.105, f32[16,128,128]{2,1,0:T(8,128)} %get-tuple-element.82), kind=kOutput, calls=%fused_computation.14 | convolution fusion | flops 407633920 | bytes 13631488 | tf_op jit(solution)/shard_map/aro,rbo->arb/dot_general | solution.py:67
  311.6 4.6 %copy.36 = bf16[768,2048]{1,0:T(8,128)(2,1)} copy(bf16[768,2048]{0,1:T(8,128)(2,1)} %bitcast.106) | data formatting | bytes 6291456
  (17 shorter events, 24.0 us)
Async XLA Ops:
  7.2 1.9 copy-start
  7.2 120.7 %all-gather.5.cloned.1.call-start = ((), (), s32[]{:S(2)}) async-start(), calls=%async_computation | async-start | bytes 17825792 | tf_op jit(solution)/shard_map/all_gather | solution.py:14
  13.3 228.2 %all-gather.7.cloned.1.call-start = ((), (), s32[]{:S(2)}) async-start(), calls=%async_computation.1 | async-start | bytes 17825792 | tf_op jit(solution)/shard_map/all_gather | solution.py:14
Sparse Core Ops, SparseCore 0:
  13.5 114.3 all-gather.4
  130.6 110.8 all-gather.6
where the time goes:
time: 324 us; the launch traced here: 323 us
  waiting for transfers between devices  166 us (51%)
  matrix products  78.6 us (24%)
  other arithmetic  41.3 us (13%)
  local copies, waits for them, and re-layouts  22.6 us (7%)
  between operations  14.1 us (4%)
    all_gather x2, waiting for transfers between devices, carried_in(): gathered = lax.all_gather(part, axis)  166 us
    add x15, other arithmetic, add_states(): return earlier + later_state  40.3 us
    unnamed x5, local copies, waits for them, and re-layouts  15.7 us
    dot_general x1, matrix products, on_device(): jnp.einsum('eca,ceo->aeo', weight_gradients, query_token_rows, preferred_...  13.3 us
    dot_general x1, matrix products, on_device(): jnp.einsum('ynv,vyq->nyq', weight_gradients, lookup_per_position, preferr...  12.7 us
    dot_general x1, matrix products, on_device(): jnp.einsum('uno,nud->oud', forward_weight_matrix, gradient_token_rows, pr...  12.4 us
    dot_general x1, matrix products, on_device(): jnp.einsum('thv,shv->hts', gradient_token_rows, content_per_position, pre...  11.8 us
    dot_general x1, matrix products, on_device(): jnp.einsum('nam,amx->nax', lookup_per_position, suffix_halves, preferred_...  6.92 us
  transfers between devices with their start and end apart: 2, of which 2 were waited for; matrix products, arithmetic and copies ran while one was open for 19% of the time, Pallas kernels for 0%

commit v1 on v0

v1 whole, which is shorter than its diff:
```python
import functools

import jax
import jax.numpy as jnp
from jax import lax
from jax.experimental import pallas as pl
from jax.experimental.pallas import tpu as pltpu
from jax.sharding import PartitionSpec as P

HEADS = 16
HEAD_DIM = 128
CHUNK = 256
MESH = pl.DeviceIdType.MESH
F32 = jnp.float32
BF16 = jnp.bfloat16


def mm(a, b):
    return lax.dot_general(a, b, (((1,), (0,)), ((), ())), preferred_element_type=F32)


def mm_nt(a, b):
    return lax.dot_general(a, b, (((1,), (1,)), ((), ())), preferred_element_type=F32)


def mm_tn(a, b):
    return lax.dot_general(a, b, (((0,), (0,)), ((), ())), preferred_element_type=F32)


def kernel(
    scale,
    count,
    early,
    q_hbm,
    k_hbm,
    v_hbm,
    g_hbm,
    dq_ref,
    dk_ref,
    dv_ref,
    q_ref,
    k_ref,
    v_ref,
    g_ref,
    pq_ref,
    pk_ref,
    pv_ref,
    sums,
    parts,
    gathered,
    scans,
    states,
    load_sem,
    send_a,
    recv_a,
    send_b,
    recv_b,
):
    me = lax.axis_index("seq")
    rows = q_ref.shape[0]
    chunks = rows // CHUNK

    def peer(step):
        return lax.rem(me + step, count)

    def lanes(head):
        return pl.ds(pl.multiple_of(head * HEAD_DIM, HEAD_DIM), HEAD_DIM)

    barrier = pltpu.get_barrier_semaphore()

    def greet(step, carry):
        pl.semaphore_signal(barrier, inc=1, device_id={"seq": peer(step)}, device_id_type=MESH)
        return carry

    lax.fori_loop(1, count, greet, 0)

    def load(which, head):
        source = (k_hbm, v_hbm, q_hbm, g_hbm)[which]
        target = (k_ref, v_ref, q_ref, g_ref)[which]
        return pltpu.make_async_copy(
            source.at[:, lanes(head)], target.at[:, lanes(head)], load_sem.at[which, head]
        )

    for pair in ((0, 1), (2, 3)):

        def begin(step, carry):
            for which in pair:
                load(which, peer(step)).start()
            return carry

        lax.fori_loop(1, count + 1, begin, 0)

    def to_hub(kind, head):
        return pltpu.make_async_remote_copy(
            src_ref=sums.at[kind, head],
            dst_ref=gathered.at[kind, me],
            send_sem=send_a.at[kind, head],
            recv_sem=recv_a.at[kind, me],
            device_id={"seq": head},
            device_id_type=MESH,
        )

    def from_source(kind, source):
        return pltpu.make_async_remote_copy(
            src_ref=sums.at[kind, source],
            dst_ref=gathered.at[kind, source],
            send_sem=send_a.at[kind, source],
            recv_sem=recv_a.at[kind, source],
            device_id={"seq": source},
            device_id_type=MESH,
        )

    def to_owner(kind, owner):
        return pltpu.make_async_remote_copy(
            src_ref=scans.at[kind, owner],
            dst_ref=states.at[kind, me],
            send_sem=send_b.at[kind, owner],
            recv_sem=recv_b.at[kind, me],
            device_id={"seq": owner},
            device_id_type=MESH,
        )

    def from_hub(kind, hub):
        return pltpu.make_async_remote_copy(
            src_ref=scans.at[kind, hub],
            dst_ref=states.at[kind, hub],
            send_sem=send_b.at[kind, hub],
            recv_sem=recv_b.at[kind, hub],
            device_id={"seq": hub},
            device_id_type=MESH,
        )

    def reduce_head(kind, head):
        left = (k_ref, q_ref)[kind]
        right = (v_ref, g_ref)[kind]
        for which in ((0, 1), (2, 3))[kind]:
            load(which, head).wait()
        total = None
        for step in range(chunks):
            chunk = step if kind == 0 else chunks - 1 - step
            here = pl.ds(chunk * CHUNK, CHUNK)
            term = mm_tn(left[here, lanes(head)], right[here, lanes(head)])
            total = term if total is None else total + term
            if step < chunks - 1:
                parts[kind, step, head] = total
        return total

    for kind in (0, 1):
        if kind == 0:
            head = peer(1)
            sums[kind, head] = reduce_head(kind, head)
            pl.semaphore_wait(barrier, count - 1)
            to_hub(kind, head).start()

        def send_sums(step, carry):
            head = peer(step)
            sums[kind, head] = reduce_head(kind, head)
            to_hub(kind, head).start()
            return carry

        lax.fori_loop(2 - kind, count, send_sums, 0)
        gathered[kind, me] = reduce_head(kind, me)

    later = lax.broadcasted_iota(jnp.int32, (CHUNK, CHUNK), 0)
    sooner = lax.broadcasted_iota(jnp.int32, (CHUNK, CHUNK), 1)

    def within(head, carry):
        for chunk in range(chunks):
            here = pl.ds(chunk * CHUNK, CHUNK)
            q = q_ref[here, lanes(head)]
            k = k_ref[here, lanes(head)]
            v = v_ref[here, lanes(head)]
            g = g_ref[here, lanes(head)]
            weights = jnp.where(later >= sooner, scale * mm_nt(g, v), 0.0).astype(BF16)
            pq_ref[here, lanes(head)] = mm(weights, k)
            turned = jnp.where(later <= sooner, scale * mm_nt(v, g), 0.0).astype(BF16)
            pk_ref[here, lanes(head)] = mm(turned, q)
            forward = jnp.where(later <= sooner, scale * mm_nt(k, q), 0.0).astype(BF16)
            pv_ref[here, lanes(head)] = mm(forward, g)
        return carry

    def scan(kind):
        def arrive(step, carry):
            from_source(kind, peer(step)).wait_recv()
            return carry

        lax.fori_loop(1, count, arrive, 0)

        def add(step, carry):
            source = step if kind == 0 else count - 1 - step
            scans[kind, source] = carry
            return carry + gathered[kind, source]

        lax.fori_loop(0, count, add, jnp.zeros((HEAD_DIM, HEAD_DIM), F32))
        states[kind, me] = scans[kind, me]

        def give(step, carry):
            to_owner(kind, peer(step)).start()
            return carry

        lax.fori_loop(1, count, give, 0)

    lax.fori_loop(0, early, within, 0)
    scan(0)
    lax.fori_loop(early, HEADS, within, 0)
    scan(1)

    def state_at(kind, head, step):
        state = states[kind, head]
        if step > 0:
            state = state + parts[kind, step - 1, head]
        return state.astype(BF16)

    def finish_q(head):
        for chunk in range(chunks):
            here = pl.ds(chunk * CHUNK, CHUNK)
            carried = mm_nt(g_ref[here, lanes(head)], state_at(0, head, chunk))
            dq_ref[here, lanes(head)] = (pq_ref[here, lanes(head)] + scale * carried).astype(BF16)

    def finish_kv(head):
        for chunk in range(chunks):
            here = pl.ds(chunk * CHUNK, CHUNK)
            state = state_at(1, head, chunks - 1 - chunk)
            carried = mm_nt(v_ref[here, lanes(head)], state)
            dk_ref[here, lanes(head)] = (pk_ref[here, lanes(head)] + scale * carried).astype(BF16)
            carried = mm(k_ref[here, lanes(head)], state)
            dv_ref[here, lanes(head)] = (pv_ref[here, lanes(head)] + scale * carried).astype(BF16)

    for kind, finish in ((0, finish_q), (1, finish_kv)):
        finish(me)

        def settle(step, carry):
            head = peer(count - step)
            from_hub(kind, head).wait_recv()
            finish(head)
            return carry

        lax.fori_loop(1, count, settle, 0)

    for kind in (0, 1):

        def sent(step, carry):
            to_hub(kind, peer(step)).wait_send()
            to_owner(kind, peer(step)).wait_send()
            return carry

        lax.fori_loop(1, count, sent, 0)


def on_device(queries, key_rows, value_rows, out_grad):
    rows, width = queries.shape
    count = lax.axis_size("seq")
    scale = (HEAD_DIM * rows * count) ** (-0.5)
    wide = (rows, width)
    square = (HEAD_DIM, HEAD_DIM)
    chunks = rows // CHUNK
    return pl.pallas_call(
        functools.partial(kernel, scale, count, 10),
        name="layer",
        out_shape=[OUT(wide, BF16)] * 3,
        in_specs=[pl.BlockSpec(memory_space=pl.ANY)] * 4,
        out_specs=[pl.BlockSpec(memory_space=pltpu.VMEM)] * 3,
        scratch_shapes=[pltpu.VMEM(wide, BF16)] * 4
        + [pltpu.VMEM(wide, F32)] * 3
        + [
            pltpu.VMEM((2, HEADS) + square, F32),
            pltpu.VMEM((2, chunks - 1, HEADS) + square, F32),
            pltpu.VMEM((2, count) + square, F32),
            pltpu.VMEM((2, count) + square, F32),
            pltpu.VMEM((2, HEADS) + square, F32),
            pltpu.SemaphoreType.DMA((4, HEADS)),
            pltpu.SemaphoreType.DMA((2, HEADS)),
            pltpu.SemaphoreType.DMA((2, count)),
            pltpu.SemaphoreType.DMA((2, count)),
            pltpu.SemaphoreType.DMA((2, HEADS)),
        ],
        compiler_params=pltpu.CompilerParams(
            collective_id=0, has_side_effects=True, vmem_limit_bytes=62 << 20
        ),
    )(queries, key_rows, value_rows, out_grad)


OUT = jax.ShapeDtypeStruct


def solution(mesh):
    placed = P(("lists", "seq"), None)
    return jax.shard_map(
        on_device,
        mesh=mesh,
        in_specs=(placed,) * 4,
        out_specs=(placed,) * 3,
        check_vma=False,
    )
```

time: 324 us -> 71.7 us (0.22)
  waiting for transfers between devices: 166 us -> 0 us
  matrix products: 78.6 us -> 0 us
  Pallas kernels: 0 us -> 62 us
  other arithmetic: 41.3 us -> 0 us
  local copies, waits for them, and re-layouts: 22.6 us -> 8.81 us
  between operations: 14.1 us -> 0.65 us
    all_gather x2 -> x0, waiting for transfers between devices: 166 us -> none  [carried_in(): gathered = lax.all_gather(part, axis)]
    dot_general x9 -> x0, matrix products: 78.6 us -> none  [the longest x1 13.3 us: on_device(): jnp.einsum('eca,ceo->aeo', weight_gradients, query_token_rows, preferred_...]
    pallas_call x0 -> x1, Pallas kernels: none -> 62 us  [on_device(): pl.pallas_call(functools.partial(kernel, scale, count, 10), name='layer',...]
    add x15 -> x0, other arithmetic: 40.3 us -> none  [add_states(): return earlier + later_state]
    unnamed x5 -> x7, local copies, waits for them, and re-layouts: 15.7 us -> 8.81 us
    reshape x1 -> x0, local copies, waits for them, and re-layouts: 4.64 us -> none  [on_device(): gradient_token_rows = out_grad.reshape(shape3)]
  transfers between devices with their start and end apart: 2 -> 0, of which waited for: 2 -> 0; matrix products, arithmetic and copies ran while one was open for 19% -> 0% of each run, Pallas kernels for 0% -> 0%
where the time goes in v1:
time: 71.7 us; the launch traced here: 71.5 us
  Pallas kernels  62 us (86%)
  local copies, waits for them, and re-layouts  8.81 us (12%)
    pallas_call x1, Pallas kernels, on_device(): pl.pallas_call(functools.partial(kernel, scale, count, 10), name='layer',...  62 us
    unnamed x7, local copies, waits for them, and re-layouts  8.81 us

profile of v1, /device:TPU:1, one launch (start us, length us, event | category | flops | bytes accessed | tf_op | source)
XLA Modules:
  0.0 71.5 jit_solution(14379924872593626163)
XLA Ops:
  0.6 62.0 %layer.1 = (bf16[768,2048]{1,0:T(8,128)(2,1)}, bf16[768,2048]{1,0:T(8,128)(2,1)}, bf16[768,2048]{1,0:T(8,128)(2,1)}) custom-call(bf16[768,2048]{1,0:T(8,128)(2,1)} %q_hbm.1, bf16[768,2048]{1,0:T(8,128)(2,1)} %k_hbm.1, bf16[768,2048]{1,0:T(8,128)(2,1)} %v_hbm.1, bf16[768,2048]{1,0:T(8,128)(2,1)} %g_hbm.1), custom_call_target="tpu_custom_call" | custom-call | tf_op jit(solution)/shard_map/layer/pallas_call | solution.py:257
  62.7 0.0 copy-start.1
  62.7 4.1 %copy.10 = bf16[768,2048]{1,0:T(8,128)(2,1)} copy(bf16[768,2048]{1,0:T(8,128)(2,1)} %get-tuple-element.6) | data formatting | bytes 6291456
  66.8 0.0 copy-done.1
  66.8 0.0 copy-start
  66.8 1.7 %copy.11 = bf16[768,2048]{1,0:T(8,128)(2,1)} copy(bf16[768,2048]{1,0:T(8,128)(2,1)S(1)} %copy-done.1) | data formatting | bytes 6291456
  68.5 1.4 %copy-done = bf16[768,2048]{1,0:T(8,128)(2,1)S(1)} copy-done((bf16[768,2048]{1,0:T(8,128)(2,1)S(1)}, bf16[768,2048]{1,0:T(8,128)(2,1)}, u32[]{:S(2)}) %copy-start) | copy-done | bytes 3145752
  69.8 1.7 %copy.12 = bf16[768,2048]{1,0:T(8,128)(2,1)} copy(bf16[768,2048]{1,0:T(8,128)(2,1)S(1)} %copy-done) | data formatting | bytes 6291456
Async XLA Ops:
  62.7 4.1 %copy-start.1 = (bf16[768,2048]{1,0:T(8,128)(2,1)S(1)}, bf16[768,2048]{1,0:T(8,128)(2,1)}, u32[]{:S(2)}) copy-start(bf16[768,2048]{1,0:T(8,128)(2,1)} %get-tuple-element.7) | copy-start | bytes 9437188
  66.8 3.0 %copy-start = (bf16[768,2048]{1,0:T(8,128)(2,1)S(1)}, bf16[768,2048]{1,0:T(8,128)(2,1)}, u32[]{:S(2)}) copy-start(bf16[768,2048]{1,0:T(8,128)(2,1)} %get-tuple-element.8) | copy-start | bytes 9437188

commit v2 on v1

--- a/solution.py
+++ b/solution.py
@@ -74,21 +74,27 @@
 
     lax.fori_loop(1, count, greet, 0)
 
-    def load(which, head):
+    def pair_at(step):
+        return lax.rem(me // 2 + step, HEADS // 2)
+
+    def wide_lanes(pair):
+        return pl.ds(pl.multiple_of(pair * 2 * HEAD_DIM, 2 * HEAD_DIM), 2 * HEAD_DIM)
+
+    def load(which, pair):
         source = (k_hbm, v_hbm, q_hbm, g_hbm)[which]
         target = (k_ref, v_ref, q_ref, g_ref)[which]
         return pltpu.make_async_copy(
-            source.at[:, lanes(head)], target.at[:, lanes(head)], load_sem.at[which, head]
-        )
-
-    for pair in ((0, 1), (2, 3)):
+            source.at[:, wide_lanes(pair)], target.at[:, wide_lanes(pair)], load_sem.at[which, pair]
+        )
+
+    for first in (0, 2):
 
         def begin(step, carry):
-            for which in pair:
-                load(which, peer(step)).start()
-            return carry
-
-        lax.fori_loop(1, count + 1, begin, 0)
+            load(first, pair_at(step)).start()
+            load(first + 1, pair_at(step)).start()
+            return carry
+
+        lax.fori_loop(1, HEADS // 2 + 1, begin, 0)
 
     def to_hub(kind, head):
         return pltpu.make_async_remote_copy(
@@ -130,36 +136,46 @@
             device_id_type=MESH,
         )
 
-    def reduce_head(kind, head):
+    def reduce_pair(kind, pair):
         left = (k_ref, q_ref)[kind]
         right = (v_ref, g_ref)[kind]
-        for which in ((0, 1), (2, 3))[kind]:
-            load(which, head).wait()
+        load(2 * kind, pair).wait()
+        load(2 * kind + 1, pair).wait()
         total = None
         for step in range(chunks):
             chunk = step if kind == 0 else chunks - 1 - step
             here = pl.ds(chunk * CHUNK, CHUNK)
-            term = mm_tn(left[here, lanes(head)], right[here, lanes(head)])
-            total = term if total is None else total + term
-            if step < chunks - 1:
-                parts[kind, step, head] = total
-        return total
+            both = mm_tn(left[here, wide_lanes(pair)], right[here, wide_lanes(pair)])
+            term = (both[:HEAD_DIM, :HEAD_DIM], both[HEAD_DIM:, HEAD_DIM:])
+            total = term if total is None else (total[0] + term[0], total[1] + term[1])
+            for one in (0, 1):
+                if step < chunks - 1:
+                    parts[kind, step, 2 * pair + one] = total[one]
+                else:
+                    sums[kind, 2 * pair + one] = total[one]
 
     for kind in (0, 1):
-        if kind == 0:
-            head = peer(1)
-            sums[kind, head] = reduce_head(kind, head)
-            pl.semaphore_wait(barrier, count - 1)
-            to_hub(kind, head).start()
 
         def send_sums(step, carry):
-            head = peer(step)
-            sums[kind, head] = reduce_head(kind, head)
-            to_hub(kind, head).start()
-            return carry
-
-        lax.fori_loop(2 - kind, count, send_sums, 0)
-        gathered[kind, me] = reduce_head(kind, me)
+            pair = pair_at(step)
+            reduce_pair(kind, pair)
+            if kind == 0:
+
+                @pl.when(step == 1)
+                def _():
+                    pl.semaphore_wait(barrier, count - 1)
+
+            for one in (0, 1):
+                head = 2 * pair + one
+
+                @pl.when(head != me)
+                def _():
+                    to_hub(kind, head).start()
+
+            return carry
+
+        lax.fori_loop(1, HEADS // 2 + 1, send_sums, 0)
+        gathered[kind, me] = sums[kind, me]
 
     later = lax.broadcasted_iota(jnp.int32, (CHUNK, CHUNK), 0)
     sooner = lax.broadcasted_iota(jnp.int32, (CHUNK, CHUNK), 1)
@@ -257,7 +273,7 @@
     return pl.pallas_call(
         functools.partial(kernel, scale, count, 10),
         name="layer",
-        out_shape=[OUT(wide, BF16)] * 3,
+        out_shape=[pltpu.VMEM(wide, BF16)] * 3,
         in_specs=[pl.BlockSpec(memory_space=pl.ANY)] * 4,
         out_specs=[pl.BlockSpec(memory_space=pltpu.VMEM)] * 3,
         scratch_shapes=[pltpu.VMEM(wide, BF16)] * 4
@@ -275,12 +291,9 @@
             pltpu.SemaphoreType.DMA((2, HEADS)),
         ],
         compiler_params=pltpu.CompilerParams(
-            collective_id=0, has_side_effects=True, vmem_limit_bytes=62 << 20
+            collective_id=0, has_side_effects=True, vmem_limit_bytes=48 << 20
         ),
     )(queries, key_rows, value_rows, out_grad)
-
-
-OUT = jax.ShapeDtypeStruct
 
 
 def solution(mesh):

time: 71.7 us -> 63.6 us (0.89)
  Pallas kernels: 62 us -> 57.8 us
  local copies, waits for them, and re-layouts: 8.81 us -> 4.99 us
    pallas_call x1, Pallas kernels: 62 us -> 57.8 us  [on_device(): pl.pallas_call(functools.partial(kernel, scale, count, 10), name='layer',...]
    unnamed x7 -> x3, local copies, waits for them, and re-layouts: 8.81 us -> 4.99 us
where the time goes in v2:
time: 63.6 us; the launch traced here: 63.4 us
  Pallas kernels  57.8 us (91%)
  local copies, waits for them, and re-layouts  4.99 us (8%)
  between operations  0.64 us (1%)
    pallas_call x1, Pallas kernels, on_device(): pl.pallas_call(functools.partial(kernel, scale, count, 10), name='layer',...  57.8 us
    unnamed x3, local copies, waits for them, and re-layouts  4.99 us

profile of v2, /device:TPU:1, one launch (start us, length us, event | category | flops | bytes accessed | tf_op | source)
XLA Modules:
  0.0 63.4 jit_solution(13791981520984657545)
XLA Ops:
  0.6 57.8 %layer.1 = (bf16[768,2048]{1,0:T(8,128)(2,1)S(1)}, bf16[768,2048]{1,0:T(8,128)(2,1)S(1)}, bf16[768,2048]{1,0:T(8,128)(2,1)S(1)}) custom-call(bf16[768,2048]{1,0:T(8,128)(2,1)} %q_hbm.1, bf16[768,2048]{1,0:T(8,128)(2,1)} %k_hbm.1, bf16[768,2048]{1,0:T(8,128)(2,1)} %v_hbm.1, bf16[768,2048]{1,0:T(8,128)(2,1)} %g_hbm.1), custom_call_target="tpu_custom_call" | custom-call | tf_op jit(solution)/shard_map/layer/pallas_call | solution.py:273
  58.5 1.7 %copy.10 = bf16[768,2048]{1,0:T(8,128)(2,1)} copy(bf16[768,2048]{1,0:T(8,128)(2,1)S(1)} %get-tuple-element.3) | data formatting | bytes 6291456
  60.1 1.7 %copy.11 = bf16[768,2048]{1,0:T(8,128)(2,1)} copy(bf16[768,2048]{1,0:T(8,128)(2,1)S(1)} %get-tuple-element.4) | data formatting | bytes 6291456
  61.8 1.7 %copy.12 = bf16[768,2048]{1,0:T(8,128)(2,1)} copy(bf16[768,2048]{1,0:T(8,128)(2,1)S(1)} %get-tuple-element.5) | data formatting | bytes 6291456

commit v3 on v2

--- a/solution.py
+++ b/solution.py
@@ -11,6 +11,11 @@
 HEAD_DIM = 128
 CHUNK = 256
 MESH = pl.DeviceIdType.MESH
+ORDER = (
+    (1, 0), (0, 1), (-1, 0), (0, -1), (1, 1), (-1, -1), (1, -1), (-1, 1),
+    (2, 0), (0, 2), (2, 1), (1, 2), (2, -1), (-1, 2), (2, 2),
+)
+SIDE = 4
 F32 = jnp.float32
 BF16 = jnp.bfloat16
 
@@ -63,6 +68,11 @@
     def peer(step):
         return lax.rem(me + step, count)
 
+    def toward(dx, dy):
+        x = lax.rem(lax.rem(me, SIDE) + dx + SIDE, SIDE)
+        y = lax.rem(lax.div(me, SIDE) + dy + SIDE, SIDE)
+        return y * SIDE + x
+
     def lanes(head):
         return pl.ds(pl.multiple_of(head * HEAD_DIM, HEAD_DIM), HEAD_DIM)
 
@@ -156,25 +166,15 @@
 
     for kind in (0, 1):
 
-        def send_sums(step, carry):
-            pair = pair_at(step)
-            reduce_pair(kind, pair)
-            if kind == 0:
-
-                @pl.when(step == 1)
-                def _():
-                    pl.semaphore_wait(barrier, count - 1)
-
-            for one in (0, 1):
-                head = 2 * pair + one
-
-                @pl.when(head != me)
-                def _():
-                    to_hub(kind, head).start()
-
+        def add_pair(step, carry):
+            reduce_pair(kind, pair_at(step))
             return carry
 
-        lax.fori_loop(1, HEADS // 2 + 1, send_sums, 0)
+        lax.fori_loop(1, HEADS // 2 + 1, add_pair, 0)
+        if kind == 0:
+            pl.semaphore_wait(barrier, count - 1)
+        for dx, dy in ORDER:
+            to_hub(kind, toward(dx, dy)).start()
         gathered[kind, me] = sums[kind, me]
 
     later = lax.broadcasted_iota(jnp.int32, (CHUNK, CHUNK), 0)
@@ -210,11 +210,8 @@
         lax.fori_loop(0, count, add, jnp.zeros((HEAD_DIM, HEAD_DIM), F32))
         states[kind, me] = scans[kind, me]
 
-        def give(step, carry):
-            to_owner(kind, peer(step)).start()
-            return carry
-
-        lax.fori_loop(1, count, give, 0)
+        for dx, dy in ORDER:
+            to_owner(kind, toward(dx, dy)).start()
 
     lax.fori_loop(0, early, within, 0)
     scan(0)
@@ -245,22 +242,28 @@
     for kind, finish in ((0, finish_q), (1, finish_kv)):
         finish(me)
 
-        def settle(step, carry):
-            head = peer(count - step)
+        for dx, dy in ORDER:
+            head = toward(-dx, -dy)
             from_hub(kind, head).wait_recv()
             finish(head)
-            return carry
-
-        lax.fori_loop(1, count, settle, 0)
 
     for kind in (0, 1):
-
-        def sent(step, carry):
-            to_hub(kind, peer(step)).wait_send()
-            to_owner(kind, peer(step)).wait_send()
-            return carry
-
-        lax.fori_loop(1, count, sent, 0)
+        for dx, dy in ORDER:
+            to_hub(kind, toward(dx, dy)).wait_send()
+        for dx, dy in ORDER:
+            to_owner(kind, toward(dx, dy)).wait_send()
+
+
+def store_kernel(dq_ref, dk_ref, dv_ref, dq_hbm, dk_hbm, dv_hbm, sems):
+    copies = []
+    for i, (source, target) in enumerate(
+        ((dq_ref, dq_hbm), (dk_ref, dk_hbm), (dv_ref, dv_hbm))
+    ):
+        copies.append(pltpu.make_async_copy(source, target, sems.at[i]))
+    for copy in copies:
+        copy.start()
+    for copy in copies:
+        copy.wait()
 
 
 def on_device(queries, key_rows, value_rows, out_grad):
@@ -270,7 +273,7 @@
     wide = (rows, width)
     square = (HEAD_DIM, HEAD_DIM)
     chunks = rows // CHUNK
-    return pl.pallas_call(
+    grads = pl.pallas_call(
         functools.partial(kernel, scale, count, 10),
         name="layer",
         out_shape=[pltpu.VMEM(wide, BF16)] * 3,
@@ -294,6 +297,15 @@
             collective_id=0, has_side_effects=True, vmem_limit_bytes=48 << 20
         ),
     )(queries, key_rows, value_rows, out_grad)
+    return pl.pallas_call(
+        store_kernel,
+        name="store",
+        out_shape=[jax.ShapeDtypeStruct(wide, BF16)] * 3,
+        in_specs=[pl.BlockSpec(memory_space=pltpu.VMEM)] * 3,
+        out_specs=[pl.BlockSpec(memory_space=pl.ANY)] * 3,
+        scratch_shapes=[pltpu.SemaphoreType.DMA((3,))],
+        compiler_params=pltpu.CompilerParams(vmem_limit_bytes=1 << 20),
+    )(*grads)
 
 
 def solution(mesh):

time: 63.6 us -> 62.3 us (0.980)
  local copies, waits for them, and re-layouts: 4.99 us -> 0 us
  Pallas kernels: 57.8 us -> 61.5 us
    unnamed x3 -> x0, local copies, waits for them, and re-layouts: 4.99 us -> none
    pallas_call x0 -> x1, Pallas kernels: none -> 3.76 us  [on_device(): pl.pallas_call(store_kernel, name='store', out_shape=[jax.ShapeDtypeStruc...]
where the time goes in v3:
time: 62.3 us; the launch traced here: 62.1 us
  Pallas kernels  61.5 us (99%)
  between operations  0.64 us (1%)
    pallas_call x1, Pallas kernels, on_device(): pl.pallas_call(functools.partial(kernel, scale, count, 10), name='layer',...  57.7 us
    pallas_call x1, Pallas kernels, on_device(): pl.pallas_call(store_kernel, name='store', out_shape=[jax.ShapeDtypeStruc...  3.76 us

profile of v3, /device:TPU:1, one launch (start us, length us, event | category | flops | bytes accessed | tf_op | source)
XLA Modules:
  0.0 62.1 jit_solution(16899481076716649790)
XLA Ops:
  0.6 57.7 %layer.1 = (bf16[768,2048]{1,0:T(8,128)(2,1)S(1)}, bf16[768,2048]{1,0:T(8,128)(2,1)S(1)}, bf16[768,2048]{1,0:T(8,128)(2,1)S(1)}) custom-call(bf16[768,2048]{1,0:T(8,128)(2,1)} %q_hbm.1, bf16[768,2048]{1,0:T(8,128)(2,1)} %k_hbm.1, bf16[768,2048]{1,0:T(8,128)(2,1)} %v_hbm.1, bf16[768,2048]{1,0:T(8,128)(2,1)} %g_hbm.1), custom_call_target="tpu_custom_call" | custom-call | tf_op jit(solution)/shard_map/layer/pallas_call | solution.py:276
  58.3 3.8 %store.1 = (bf16[768,2048]{1,0:T(8,128)(2,1)}, bf16[768,2048]{1,0:T(8,128)(2,1)}, bf16[768,2048]{1,0:T(8,128)(2,1)}) custom-call(bf16[768,2048]{1,0:T(8,128)(2,1)S(1)} %get-tuple-element.6.dq_ref, bf16[768,2048]{1,0:T(8,128)(2,1)S(1)} %get-tuple-element.7.dk_ref, bf16[768,2048]{1,0:T(8,128)(2,1)S(1)} %get-tuple-element.8.dv_ref), custom_call_target="tpu_custom_call" | custom-call | tf_op jit(solution)/shard_map/store/pallas_call | solution.py:300

commit v4 on v3

--- a/solution.py
+++ b/solution.py
@@ -16,6 +16,7 @@
     (2, 0), (0, 2), (2, 1), (1, 2), (2, -1), (-1, 2), (2, 2),
 )
 SIDE = 4
+PIECES = 4
 F32 = jnp.float32
 BF16 = jnp.bfloat16
 
@@ -259,7 +260,12 @@
     for i, (source, target) in enumerate(
         ((dq_ref, dq_hbm), (dk_ref, dk_hbm), (dv_ref, dv_hbm))
     ):
-        copies.append(pltpu.make_async_copy(source, target, sems.at[i]))
+        for j in range(PIECES):
+            block = source.shape[0] // PIECES
+            piece = pl.ds(j * block, block)
+            copies.append(
+                pltpu.make_async_copy(source.at[piece], target.at[piece], sems.at[i, j])
+            )
     for copy in copies:
         copy.start()
     for copy in copies:
@@ -303,7 +309,7 @@
         out_shape=[jax.ShapeDtypeStruct(wide, BF16)] * 3,
         in_specs=[pl.BlockSpec(memory_space=pltpu.VMEM)] * 3,
         out_specs=[pl.BlockSpec(memory_space=pl.ANY)] * 3,
-        scratch_shapes=[pltpu.SemaphoreType.DMA((3,))],
+        scratch_shapes=[pltpu.SemaphoreType.DMA((3, PIECES))],
         compiler_params=pltpu.CompilerParams(vmem_limit_bytes=1 << 20),
     )(*grads)
 

time: 62.3 us -> 62.3 us (level)
  no operation moved by 1% of the time
where the time goes in v4:
time: 62.3 us; the launch traced here: 62.1 us
  Pallas kernels  61.4 us (99%)
  between operations  0.64 us (1%)
    pallas_call x1, Pallas kernels, on_device(): pl.pallas_call(functools.partial(kernel, scale, count, 10), name='layer',...  57.7 us
    pallas_call x1, Pallas kernels, on_device(): pl.pallas_call(store_kernel, name='store', out_shape=[jax.ShapeDtypeStruc...  3.72 us

profile of v4, /device:TPU:1, one launch (start us, length us, event | category | flops | bytes accessed | tf_op | source)
XLA Modules:
  0.0 62.1 jit_solution(4751937848888293213)
XLA Ops:
  0.6 57.7 %layer.1 = (bf16[768,2048]{1,0:T(8,128)(2,1)S(1)}, bf16[768,2048]{1,0:T(8,128)(2,1)S(1)}, bf16[768,2048]{1,0:T(8,128)(2,1)S(1)}) custom-call(bf16[768,2048]{1,0:T(8,128)(2,1)} %q_hbm.1, bf16[768,2048]{1,0:T(8,128)(2,1)} %k_hbm.1, bf16[768,2048]{1,0:T(8,128)(2,1)} %v_hbm.1, bf16[768,2048]{1,0:T(8,128)(2,1)} %g_hbm.1), custom_call_target="tpu_custom_call" | custom-call | tf_op jit(solution)/shard_map/layer/pallas_call | solution.py:282
  58.3 3.7 %store.1 = (bf16[768,2048]{1,0:T(8,128)(2,1)}, bf16[768,2048]{1,0:T(8,128)(2,1)}, bf16[768,2048]{1,0:T(8,128)(2,1)}) custom-call(bf16[768,2048]{1,0:T(8,128)(2,1)S(1)} %get-tuple-element.6.dq_ref, bf16[768,2048]{1,0:T(8,128)(2,1)S(1)} %get-tuple-element.7.dk_ref, bf16[768,2048]{1,0:T(8,128)(2,1)S(1)} %get-tuple-element.8.dv_ref), custom_call_target="tpu_custom_call" | custom-call | tf_op jit(solution)/shard_map/store/pallas_call | solution.py:306

commit v5 on v4

--- a/solution.py
+++ b/solution.py
@@ -69,6 +69,9 @@
     def peer(step):
         return lax.rem(me + step, count)
 
+    def unused(kind):
+        return count - 1 if kind == 0 else 0
+
     def toward(dx, dy):
         x = lax.rem(lax.rem(me, SIDE) + dx + SIDE, SIDE)
         y = lax.rem(lax.div(me, SIDE) + dy + SIDE, SIDE)
@@ -174,9 +177,19 @@
         lax.fori_loop(1, HEADS // 2 + 1, add_pair, 0)
         if kind == 0:
             pl.semaphore_wait(barrier, count - 1)
-        for dx, dy in ORDER:
-            to_hub(kind, toward(dx, dy)).start()
+
+        @pl.when(me != unused(kind))
+        def _():
+            for dx, dy in ORDER:
+                to_hub(kind, toward(dx, dy)).start()
+
         gathered[kind, me] = sums[kind, me]
+
+        @pl.when(me == unused(1 - kind))
+        def _():
+            for head in range(HEADS):
+                states[kind, head] = jnp.zeros((HEAD_DIM, HEAD_DIM), F32)
+
 
     later = lax.broadcasted_iota(jnp.int32, (CHUNK, CHUNK), 0)
     sooner = lax.broadcasted_iota(jnp.int32, (CHUNK, CHUNK), 1)
@@ -198,7 +211,12 @@
 
     def scan(kind):
         def arrive(step, carry):
-            from_source(kind, peer(step)).wait_recv()
+            source = peer(step)
+
+            @pl.when(source != unused(kind))
+            def _():
+                from_source(kind, source).wait_recv()
+
             return carry
 
         lax.fori_loop(1, count, arrive, 0)
@@ -208,11 +226,16 @@
             scans[kind, source] = carry
             return carry + gathered[kind, source]
 
-        lax.fori_loop(0, count, add, jnp.zeros((HEAD_DIM, HEAD_DIM), F32))
+        total = lax.fori_loop(0, count - 1, add, jnp.zeros((HEAD_DIM, HEAD_DIM), F32))
+        scans[kind, unused(kind)] = total
         states[kind, me] = scans[kind, me]
 
         for dx, dy in ORDER:
-            to_owner(kind, toward(dx, dy)).start()
+
+            @pl.when(toward(dx, dy) != unused(1 - kind))
+            def _():
+                to_owner(kind, toward(dx, dy)).start()
+
 
     lax.fori_loop(0, early, within, 0)
     scan(0)
@@ -245,14 +268,25 @@
 
         for dx, dy in ORDER:
             head = toward(-dx, -dy)
-            from_hub(kind, head).wait_recv()
+
+            @pl.when(me != unused(1 - kind))
+            def _():
+                from_hub(kind, head).wait_recv()
+
             finish(head)
 
     for kind in (0, 1):
+
+        @pl.when(me != unused(kind))
+        def _():
+            for dx, dy in ORDER:
+                to_hub(kind, toward(dx, dy)).wait_send()
+
         for dx, dy in ORDER:
-            to_hub(kind, toward(dx, dy)).wait_send()
-        for dx, dy in ORDER:
-            to_owner(kind, toward(dx, dy)).wait_send()
+
+            @pl.when(toward(dx, dy) != unused(1 - kind))
+            def _():
+                to_owner(kind, toward(dx, dy)).wait_send()
 
 
 def store_kernel(dq_ref, dk_ref, dv_ref, dq_hbm, dk_hbm, dv_hbm, sems):

time: 62.3 us -> 63.1 us (1.013)
  the two profiles are of different devices: /device:TPU:1 before, /device:TPU:70 now
where the time goes in v5:
time: 63.1 us; the launch traced here: 63 us
  Pallas kernels  62.3 us (99%)
  between operations  0.64 us (1%)
    pallas_call x1, Pallas kernels, on_device(): pl.pallas_call(functools.partial(kernel, scale, count, 10), name='layer',...  58.6 us
    pallas_call x1, Pallas kernels, on_device(): pl.pallas_call(store_kernel, name='store', out_shape=[jax.ShapeDtypeStruc...  3.72 us

profile of v5, /device:TPU:70, one launch (start us, length us, event | category | flops | bytes accessed | tf_op | source)
XLA Modules:
  0.0 63.0 jit_solution(17868182177913418422)
XLA Ops:
  0.6 58.6 %layer.1 = (bf16[768,2048]{1,0:T(8,128)(2,1)S(1)}, bf16[768,2048]{1,0:T(8,128)(2,1)S(1)}, bf16[768,2048]{1,0:T(8,128)(2,1)S(1)}) custom-call(bf16[768,2048]{1,0:T(8,128)(2,1)} %q_hbm.1, bf16[768,2048]{1,0:T(8,128)(2,1)} %k_hbm.1, bf16[768,2048]{1,0:T(8,128)(2,1)} %v_hbm.1, bf16[768,2048]{1,0:T(8,128)(2,1)} %g_hbm.1), custom_call_target="tpu_custom_call" | custom-call | tf_op jit(solution)/shard_map/layer/pallas_call | solution.py:316
  59.3 3.7 %store.1 = (bf16[768,2048]{1,0:T(8,128)(2,1)}, bf16[768,2048]{1,0:T(8,128)(2,1)}, bf16[768,2048]{1,0:T(8,128)(2,1)}) custom-call(bf16[768,2048]{1,0:T(8,128)(2,1)S(1)} %get-tuple-element.6.dq_ref, bf16[768,2048]{1,0:T(8,128)(2,1)S(1)} %get-tuple-element.7.dk_ref, bf16[768,2048]{1,0:T(8,128)(2,1)S(1)} %get-tuple-element.8.dv_ref), custom_call_target="tpu_custom_call" | custom-call | tf_op jit(solution)/shard_map/store/pallas_call | solution.py:340
